TPU v7x, 32 devices: a whole 2x2x4 slice. The times are simulated.
32 devices in a mesh: gx: 8 (over z, x), gy: 4 (over y, core).
Axes of the slice: x: 2, y: 2, z: 4, core: 2. Of those that a mesh axis runs over, the one named last changes fastest.
Arguments:
- inputs: bfloat16 [64, 64, 256], P('gx', 'gy'), may hold values from -6 to 6
- coarse: bfloat16 [64, 64, 256], P('gx', 'gy'), may hold values from -6 to 6
- cotangent: bfloat16 [64, 64, 256], P('gx', 'gy'), may hold values from -16 to 16
- enc_weight: bfloat16 [3, 3, 3, 32, 32], replicated, may hold values from -0.21875 to 0.21875
- dec_weight: bfloat16 [3, 3, 3, 64, 32], replicated, may hold values from -0.15625 to 0.15625
Outputs:
- inputs_grad: bfloat16 [64, 64, 256], P('gx', 'gy')
- coarse_grad: bfloat16 [64, 64, 256], P('gx', 'gy')
- enc_weight_grad: float32 [3, 3, 3, 32, 32], replicated
- dec_weight_grad: float32 [3, 3, 3, 64, 32], replicated
All inputs are finite; a program needn't handle non-finite values.
Results may differ from a plain program's by a relative error of at most 0.0059.
Values may be sent and summed in bfloat16 or wider, within the bound.
A program may use at most 64 MiB of HBM per device.

v0:
```python
import math

import jax
import jax.numpy as jnp
from jax import lax
from jax.sharding import PartitionSpec as P


def extended(cells, sides, width):
    for axis, dim in sides:
        count = lax.axis_size(axis)
        head = lax.slice_in_dim(cells, 0, width, axis=dim)
        tail = lax.slice_in_dim(cells, cells.shape[dim] - width, cells.shape[dim], axis=dim)
        cells = jnp.concatenate(
            [
                lax.ppermute(tail, axis, [(i, (i + 1) % count) for i in range(count)]),
                cells,
                lax.ppermute(head, axis, [((i + 1) % count, i) for i in range(count)]),
            ],
            axis=dim,
        )
    return cells


def shift_table(planes):
    source = lax.broadcasted_iota(jnp.int32, (3, planes, planes), 1)
    target = lax.broadcasted_iota(jnp.int32, (3, planes, planes), 2)
    offset = lax.broadcasted_iota(jnp.int32, (3, planes, planes), 0)
    return (source == target + offset - 1).astype(jnp.float32)


def make_bands(weight, planes):
    width_in = weight.shape[3]
    width_out = weight.shape[4]
    band = jnp.einsum("cpz,abcio->abpizo", shift_table(planes), weight.astype(jnp.float32))
    return band.reshape(3, 3, planes * width_in, planes * width_out).astype(jnp.bfloat16)


def band_conv(padded, band, cells_x, cells_y):
    total = None
    for shift_x in range(3):
        for shift_y in range(3):
            piece = padded[shift_x : shift_x + cells_x, shift_y : shift_y + cells_y]
            term = jnp.dot(piece, band[shift_x, shift_y], preferred_element_type=jnp.float32)
            total = term if total is None else total + term
    return total


def band_conv_back(padded, band, cells_x, cells_y):
    total = None
    for shift_x in range(3):
        for shift_y in range(3):
            piece = padded[2 - shift_x : 2 - shift_x + cells_x, 2 - shift_y : 2 - shift_y + cells_y]
            term = jnp.dot(piece, band[shift_x, shift_y].T, preferred_element_type=jnp.float32)
            total = term if total is None else total + term
    return total


def tap_sums(padded, delta, planes, width_in, width_out):
    cells_x = delta.shape[0]
    cells_y = delta.shape[1]
    flat_delta = delta.reshape(-1, delta.shape[2])
    blocks = []
    for shift_x in range(3):
        for shift_y in range(3):
            piece = padded[shift_x : shift_x + cells_x, shift_y : shift_y + cells_y].reshape(
                -1, padded.shape[2]
            )
            blocks.append(
                lax.dot_general(
                    piece, flat_delta, (((0,), (0,)), ((), ())), preferred_element_type=jnp.float32
                )
            )
    stacked = jnp.stack(blocks).reshape(3, 3, planes, width_in, planes, width_out)
    return jnp.einsum(
        "abpizo,cpz->abcio", stacked, shift_table(planes), precision=lax.Precision.HIGHEST
    )


def silu_slope(value):
    sig = jax.nn.sigmoid(value)
    return sig * (1.0 + value * (1.0 - sig))


def body(inputs, coarse, cotangent, enc_weight, dec_weight):
    cells_x = inputs.shape[0]
    cells_y = inputs.shape[1]
    channels = enc_weight.shape[3]
    planes = inputs.shape[2] // channels
    enc_band = make_bands(enc_weight, planes)
    upper_band = make_bands(dec_weight[:, :, :, :channels], planes)
    skip_band = make_bands(dec_weight[:, :, :, channels:], planes)
    scale = 1.0 / math.sqrt(cells_x * lax.axis_size("gx") * cells_y * lax.axis_size("gy") * planes)
    input_cycle = extended(inputs, (("gx", 0), ("gy", 1)), 2)
    upper_cycle = extended(coarse, (("gx", 0), ("gy", 1)), 1)
    pre_cycle = band_conv(input_cycle, enc_band, cells_x + 2, cells_y + 2)
    skip_cycle = jax.nn.silu(pre_cycle).astype(jnp.bfloat16)
    pre_dec = band_conv(upper_cycle, upper_band, cells_x, cells_y) + band_conv(
        skip_cycle, skip_band, cells_x, cells_y
    )
    dec_own = (cotangent.astype(jnp.float32) * silu_slope(pre_dec)).astype(jnp.bfloat16)
    dec_cycle = extended(dec_own, (("gx", 0), ("gy", 1)), 1)
    pre_enc = pre_cycle[1:-1, 1:-1]
    input_near = input_cycle[1:-1, 1:-1]
    coarse_grad = band_conv_back(dec_cycle, upper_band, cells_x, cells_y).astype(jnp.bfloat16)
    skip_grad = band_conv_back(dec_cycle, skip_band, cells_x, cells_y)
    enc_own = (skip_grad * silu_slope(pre_enc)).astype(jnp.bfloat16)
    enc_cycle = extended(enc_own, (("gx", 0), ("gy", 1)), 1)
    dec_terms = (
        jnp.concatenate(
            [
                tap_sums(upper_cycle, dec_own, planes, channels, channels),
                tap_sums(skip_cycle, dec_own, planes, channels, channels),
            ],
            axis=3,
        )
        * scale
    )
    inputs_grad = band_conv_back(enc_cycle, enc_band, cells_x, cells_y).astype(jnp.bfloat16)
    enc_terms = tap_sums(input_near, enc_own, planes, channels, channels) * scale
    enc_total, dec_total = lax.psum((enc_terms, dec_terms), ("gx", "gy"))
    return (inputs_grad, coarse_grad, enc_total, dec_total)


def solution(mesh):
    in_specs = (P("gx", "gy", None), P("gx", "gy", None), P("gx", "gy", None), P(), P())
    out_specs = (P("gx", "gy", None), P("gx", "gy", None), P(), P())
    return jax.shard_map(body, mesh=mesh, in_specs=in_specs, out_specs=out_specs, check_vma=False)
```

profile of v0, /device:TPU:0, one launch (start us, length us, event | category | flops | bytes accessed | tf_op | source)
XLA Modules:
  0.0 317.8 jit_solution(13585133419180768349)
XLA Ops:
  7.2 1.3 fusion.222
  8.6 2.9 collective-permute-start.4
  11.5 3.0 collective-permute-start.5
  14.5 1.3 fusion.221
  15.9 4.7 %collective-permute-start.1 = (bf16[1,16,256]{2,1,0:T(8,128)(2,1)}, bf16[1,16,256]{2,1,0:T(8,128)(2,1)}, u32[]{:S(2)}, u32[]{:S(2)}) collective-permute-start(bf16[1,16,256]{2,1,0:T(8,128)(2,1)} %get-tuple-element.39), channel_id=1, source_target_pairs={{4,0},{8,4},{12,8},{16,12},{20,16},{24,20},{28,24},{0,28},{5,1},{9... | collective-permute-start | bytes 24584 | tf_op jit(solution)/shard_map/ppermute | solution.py:18
  20.6 4.5 %convert_bitcast_fusion.1 = bf16[3,3,8,32,8,32]{5,4,3,1,0,2:T(8,128)(2,1)} fusion(bf16[3,3,3,32,32]{4,3,2,1,0:T(8,128)(2,1)} %param.8), kind=kOutput, calls=%fused_computation.1 | convolution fusion | flops 4129344 | bytes 1234944 | tf_op jit(solution)/shard_map/cpz,abcio->abpizo/dot_general | solution.py:35
  25.4 3.6 %convert_bitcast_fusion = bf16[3,3,8,32,8,32]{5,4,3,1,0,2:T(8,128)(2,1)} fusion(bf16[3,3,3,32,32]{4,2,3,1,0:T(4,128)(2,1)S(1)} %copy.56), kind=kOutput, calls=%fused_computation | convolution fusion | flops 4129344 | bytes 1234944 | tf_op jit(solution)/shard_map/cpz,abcio->abpizo/dot_general | solution.py:35
  29.3 1.7 convert_bitcast_fusion.2
  31.0 2.5 copy.33
  33.5 5.8 %convert_element_type.57 = bf16[3,3,256,256]{3,2,1,0:T(8,128)(2,1)S(1)} reshape(bf16[3,3,8,32,8,32]{5,4,3,2,1,0:T(8,128)(2,1)} %copy.33) | data formatting | bytes 2359296 | tf_op jit(solution)/shard_map/convert_element_type | solution.py:36
  40.2 5.1 %copy.35 = bf16[3,3,8,32,8,32]{5,4,3,2,1,0:T(8,128)(2,1)} copy(bf16[3,3,8,32,8,32]{5,4,3,1,0,2:T(8,128)(2,1)} %convert_bitcast_fusion.1) | data formatting | bytes 2359296 | tf_op jit(solution)/shard_map/convert_element_type | solution.py:36
  45.3 5.8 %convert_element_type.60 = bf16[3,3,256,256]{3,2,1,0:T(8,128)(2,1)S(1)} reshape(bf16[3,3,8,32,8,32]{5,4,3,2,1,0:T(8,128)(2,1)} %copy.35) | data formatting | bytes 2359296 | tf_op jit(solution)/shard_map/convert_element_type | solution.py:36
  51.1 5.1 %copy.37 = bf16[3,3,8,32,8,32]{5,4,3,2,1,0:T(8,128)(2,1)} copy(bf16[3,3,8,32,8,32]{5,4,3,1,0,2:T(8,128)(2,1)} %convert_bitcast_fusion) | data formatting | bytes 2359296 | tf_op jit(solution)/shard_map/convert_element_type | solution.py:36
  56.2 5.8 %convert_element_type.64 = bf16[3,3,256,256]{3,2,1,0:T(8,128)(2,1)S(1)} reshape(bf16[3,3,8,32,8,32]{5,4,3,2,1,0:T(8,128)(2,1)} %copy.37) | data formatting | bytes 2359296 | tf_op jit(solution)/shard_map/convert_element_type | solution.py:36
  65.3 2.6 collective-permute-done.2
  70.8 2.2 collective-permute-done.6
  74.7 1.0 multiply_convert_fusion
  79.8 0.9 fusion.14
  81.0 1.7 collective-permute-start.8
  82.8 0.9 fusion.13
  83.7 0.9 fusion.12
  84.6 0.9 fusion.11
  85.5 0.9 fusion.10
  86.4 0.9 fusion.9
  87.3 0.9 fusion.8
  88.2 0.9 fusion.7
  89.2 0.9 fusion.6
  90.1 6.7 %reshape.15 = f32[3,3,8,32,8,32]{5,4,3,2,1,0:T(8,128)} reshape(f32[9,256,256]{2,1,0:T(8,128)} %fusion.6) | data formatting | bytes 4718592 | tf_op jit(solution)/shard_map/reshape | solution.py:74
  96.8 8.8 %convolution_bitcast_fusion = f32[3,3,3,32,32]{4,2,3,1,0:T(4,128)} fusion(f32[3,3,8,32,8,32]{5,4,3,2,1,0:T(8,128)} %reshape.15), kind=kOutput, calls=%fused_computation.3 | convolution fusion | flops 21234240 | bytes 2469888 | tf_op jit(solution)/shard_map/abpizo,cpz->abcio/dot_general | solution.py:75
  105.6 2.0 copy.44
  107.6 1.9 fusion.21
  109.5 1.8 fusion.3
  111.3 0.9 fusion.20
  112.3 0.9 fusion.19
  113.2 0.9 fusion.18
  114.1 0.9 fusion.17
  115.0 0.9 fusion.16
  115.9 0.9 fusion.2
  116.8 0.9 fusion.15
  117.8 6.7 %reshape.14 = f32[3,3,8,32,8,32]{5,4,3,2,1,0:T(8,128)} reshape(f32[9,256,256]{2,1,0:T(8,128)} %fusion.15) | data formatting | bytes 4718592 | tf_op jit(solution)/shard_map/reshape | solution.py:74
  124.5 8.8 %convolution_bitcast_fusion.1 = f32[3,3,3,32,32]{4,2,3,1,0:T(4,128)} fusion(f32[3,3,8,32,8,32]{5,4,3,2,1,0:T(8,128)} %reshape.14), kind=kOutput, calls=%fused_computation.4 | convolution fusion | flops 21234240 | bytes 2469888 | tf_op jit(solution)/shard_map/abpizo,cpz->abcio/dot_general | solution.py:75
  133.3 2.0 copy.43
  135.3 2.2 maximum_multiply_fusion
  139.7 0.9 fusion.101
  140.6 1.6 fusion.84
  142.1 1.5 fusion.75
  149.2 3.0 collective-permute-start.13
  152.3 0.9 fusion.28
  153.2 1.6 fusion.5
  154.8 0.9 fusion.27
  155.8 0.9 fusion.26
  156.7 0.9 fusion.25
  157.6 0.9 fusion.24
  158.5 0.9 fusion.23
  159.4 0.9 fusion.4
  160.4 0.9 fusion.22
  161.3 6.7 %reshape.9 = f32[3,3,8,32,8,32]{5,4,3,2,1,0:T(8,128)} reshape(f32[9,256,256]{2,1,0:T(8,128)} %fusion.22) | data formatting | bytes 4718592 | tf_op jit(solution)/shard_map/reshape | solution.py:74
  168.1 8.8 %fusion.1 = f32[3,3,3,32,32]{4,2,3,1,0:T(4,128)} fusion(f32[3,3,8,32,8,32]{5,4,3,2,1,0:T(8,128)} %reshape.9), kind=kOutput, calls=%fused_computation.7 | convolution fusion | flops 21261888 | bytes 2469888 | tf_op jit(solution)/shard_map/abpizo,cpz->abcio/dot_general | solution.py:75
  177.0 1.2 fusion.58
  179.3 1.3 collective-permute-start.14
  181.0 1.0 collective-permute-done.14
  182.0 1.7 collective-permute-done.15
  185.7 122.6 %all-reduce.3.cloned.1.call-done = (f32[3,3,3,32,32]{4,2,3,1,0:T(4,128)}, f32[3,3,3,64,32]{3,4,2,1,0:T(8,128)}) async-done(((f32[3,3,3,32,32]{4,2,3,1,0:T(4,128)}, f32[3,3,3,64,32]{3,4,2,1,0:T(8,128)}), (f32[3,3,3,32,32]{4,2,3,1,0:T(4,128)}, f32[3,3,3,64,32]{3,4,2,1,0:T(8,128)})) %all-reduce.3.cloned.1.call-update) | async-done | bytes 331792 | tf_op jit(solution)/shard_map/psum | solution.py:121
  308.3 1.9 copy.45
  (172 shorter events, 25.2 us)
Async XLA Ops:
  7.2 301.1 %all-reduce.3.cloned.1.call-start = ((), (), s32[]{:S(2)}) async-start(), calls=%async_computation | async-start | bytes 2064384 | tf_op jit(solution)/shard_map/psum | solution.py:121
  8.6 60.0 %collective-permute-start.4 = (bf16[2,16,256]{2,1,0:T(8,128)(2,1)}, bf16[2,16,256]{2,1,0:T(8,128)(2,1)}, u32[]{:S(2)}, u32[]{:S(2)}) collective-permute-start(bf16[2,16,256]{2,1,0:T(8,128)(2,1)} %get-tuple-element.42), channel_id=1, source_target_pairs={{0,4},{4,8},{8,12},{12,16},{16,20},{20,24},{24,28},{28,0},{1,5},{5... | collective-permute-start | bytes 49160 | tf_op jit(solution)/shard_map/ppermute | solution.py:16
  11.5 57.8 %collective-permute-start.5 = (bf16[2,16,256]{2,1,0:T(8,128)(2,1)}, bf16[2,16,256]{2,1,0:T(8,128)(2,1)S(1)}, u32[]{:S(2)}, u32[]{:S(2)}) collective-permute-start(bf16[2,16,256]{2,1,0:T(8,128)(2,1)} %get-tuple-element.41), channel_id=1, source_target_pairs={{4,0},{8,4},{12,8},{16,12},{20,16},{24,20},{28,24},{0,28},{5,1},{9... | collective-permute-start | bytes 49160 | tf_op jit(solution)/shard_map/ppermute | solution.py:18
  15.9 46.1 %collective-permute-start = (bf16[1,16,256]{2,1,0:T(8,128)(2,1)}, bf16[1,16,256]{2,1,0:T(8,128)(2,1)}, u32[]{:S(2)}, u32[]{:S(2)}) collective-permute-start(bf16[1,16,256]{2,1,0:T(8,128)(2,1)} %get-tuple-element.40), channel_id=1, source_target_pairs={{0,4},{4,8},{8,12},{12,16},{16,20},{20,24},{24,28},{28,0},{1,5},{5... | collective-permute-start | bytes 24584 | tf_op jit(solution)/shard_map/ppermute | solution.py:16
  15.9 9.2 %copy-start.13 = (bf16[3,3,3,64,32]{3,4,2,1,0:T(8,128)(2,1)S(1)}, bf16[3,3,3,64,32]{3,4,2,1,0:T(8,128)(2,1)}, u32[]{:S(2)}) copy-start(bf16[3,3,3,64,32]{3,4,2,1,0:T(8,128)(2,1)} %param.9) | copy-start | bytes 331780
  15.9 47.7 %collective-permute-start.1 = (bf16[1,16,256]{2,1,0:T(8,128)(2,1)}, bf16[1,16,256]{2,1,0:T(8,128)(2,1)}, u32[]{:S(2)}, u32[]{:S(2)}) collective-permute-start(bf16[1,16,256]{2,1,0:T(8,128)(2,1)} %get-tuple-element.39), channel_id=1, source_target_pairs={{4,0},{8,4},{12,8},{16,12},{20,16},{24,20},{28,24},{0,28},{5,1},{9... | collective-permute-start | bytes 24584 | tf_op jit(solution)/shard_map/ppermute | solution.py:18
  33.5 5.8 %copy-start.24 = (bf16[8,16,256]{2,1,0:T(8,128)(2,1)S(1)}, bf16[8,16,256]{2,1,0:T(8,128)(2,1)}, u32[]{:S(2)}) copy-start(bf16[8,16,256]{2,1,0:T(8,128)(2,1)} %param.6) | copy-start | bytes 196612
  62.0 6.3 %copy-start.31 = (f32[8,16,256]{2,1,0:T(8,128)S(1)}, f32[8,16,256]{2,1,0:T(8,128)}, u32[]{:S(2)}) copy-start(f32[8,16,256]{2,1,0:T(8,128)} %convolution_bitcast_fusion.30) | copy-start | bytes 393220
  63.6 1.7 copy-start.34
  64.3 0.8 copy-start.26
  64.3 12.9 %copy-start.7 = (bf16[10,16,256]{2,1,0:T(8,128)(2,1)}, bf16[10,16,256]{2,1,0:T(8,128)(2,1)S(1)}, u32[]{:S(2)}) copy-start(bf16[10,16,256]{2,1,0:T(8,128)(2,1)S(1)} %get-tuple-element.46) | copy-start | bytes 245764
  64.3 3.7 %collective-permute-start.3 = (bf16[10,1,256]{2,1,0:T(2,128)(2,1)S(1)}, bf16[10,1,256]{2,1,0:T(2,128)(2,1)S(1)}, u32[]{:S(2)}, u32[]{:S(2)}) collective-permute-start(bf16[10,1,256]{2,1,0:T(2,128)(2,1)S(1)} %get-tuple-element.31), channel_id=1, source_target_pairs={{1,0},{2,1},{3,2},{0,3},{5,4},{6,5},{7,6},{4,7},{9,8},{10,9},{11,1... | collective-permute-start | bytes 15368 | tf_op jit(solution)/shard_map/ppermute | solution.py:18
  64.7 4.6 %copy-start.22 = (bf16[8,16,256]{2,1,0:T(8,128)(2,1)S(1)}, bf16[8,16,256]{2,1,0:T(8,128)(2,1)}, u32[]{:S(2)}) copy-start(bf16[8,16,256]{2,1,0:T(8,128)(2,1)} %param.5) | copy-start | bytes 196612
  64.7 3.2 %collective-permute-start.2 = (bf16[10,1,256]{2,1,0:T(2,128)(2,1)S(1)}, bf16[10,1,256]{2,1,0:T(2,128)(2,1)S(1)}, u32[]{:S(2)}, u32[]{:S(2)}) collective-permute-start(bf16[10,1,256]{2,1,0:T(2,128)(2,1)S(1)} %get-tuple-element.30), channel_id=1, source_target_pairs={{0,1},{1,2},{2,3},{3,0},{4,5},{5,6},{6,7},{7,4},{8,9},{9,10},{10,1... | collective-permute-start | bytes 15368 | tf_op jit(solution)/shard_map/ppermute | solution.py:16
  67.9 2.2 copy-start.32
  68.0 9.2 %copy-start.35 = (bf16[10,1,256]{2,1,0:T(2,128)(2,1)}, bf16[10,1,256]{2,1,0:T(2,128)(2,1)S(1)}, u32[]{:S(2)}) copy-start(bf16[10,1,256]{2,1,0:T(2,128)(2,1)S(1)} %collective-permute-done.3) | copy-start | bytes 15364
  69.3 0.6 copy-start.37
  69.3 5.4 %copy-start.3 = (bf16[12,16,256]{2,1,0:T(8,128)(2,1)}, bf16[12,16,256]{2,1,0:T(8,128)(2,1)S(1)}, u32[]{:S(2)}) copy-start(bf16[12,16,256]{2,1,0:T(8,128)(2,1)S(1)} %constant_dynamic-update-slice_fusion.7) | copy-start | bytes 294916
  69.4 1.5 collective-permute-start.7
  69.9 3.1 collective-permute-start.6
  70.8 3.6 %copy-start.29 = (bf16[12,2,256]{2,1,0:T(2,128)(2,1)}, bf16[12,2,256]{2,1,0:T(2,128)(2,1)S(1)}, u32[]{:S(2)}) copy-start(bf16[12,2,256]{2,1,0:T(2,128)(2,1)S(1)} %collective-permute-done.7) | copy-start | bytes 36868
  76.4 0.9 copy-start.39
  77.5 11.6 %copy-start = (bf16[8,16,256]{2,1,0:T(8,128)(2,1)}, bf16[8,16,256]{2,1,0:T(8,128)(2,1)S(1)}, u32[]{:S(2)}) copy-start(bf16[8,16,256]{2,1,0:T(8,128)(2,1)S(1)} %multiply_convert_fusion.1) | copy-start | bytes 196612
  80.7 56.7 %collective-permute-start.9 = (bf16[1,16,256]{2,1,0:T(8,128)(2,1)}, bf16[1,16,256]{2,1,0:T(8,128)(2,1)}, u32[]{:S(2)}, u32[]{:S(2)}) collective-permute-start(bf16[1,16,256]{2,1,0:T(8,128)(2,1)} %get-tuple-element.35), channel_id=1, source_target_pairs={{4,0},{8,4},{12,8},{16,12},{20,16},{24,20},{28,24},{0,28},{5,1},{9... | collective-permute-start | bytes 24584 | tf_op jit(solution)/shard_map/ppermute | solution.py:18
  81.0 56.4 %collective-permute-start.8 = (bf16[1,16,256]{2,1,0:T(8,128)(2,1)}, bf16[1,16,256]{2,1,0:T(8,128)(2,1)}, u32[]{:S(2)}, u32[]{:S(2)}) collective-permute-start(bf16[1,16,256]{2,1,0:T(8,128)(2,1)} %get-tuple-element.34), channel_id=1, source_target_pairs={{0,4},{4,8},{8,12},{12,16},{16,20},{20,24},{24,28},{28,0},{1,5},{5... | collective-permute-start | bytes 24584 | tf_op jit(solution)/shard_map/ppermute | solution.py:16
  107.6 3.7 %copy-start.1 = (bf16[8,16,256]{2,1,0:T(8,128)(2,1)S(1)}, bf16[8,16,256]{2,1,0:T(8,128)(2,1)}, u32[]{:S(2)}) copy-start(bf16[8,16,256]{2,1,0:T(8,128)(2,1)} %copy-done) | copy-start | bytes 196612
  107.6 3.7 %copy-start.8 = (bf16[10,16,256]{2,1,0:T(8,128)(2,1)S(1)}, bf16[10,16,256]{2,1,0:T(8,128)(2,1)}, u32[]{:S(2)}) copy-start(bf16[10,16,256]{2,1,0:T(8,128)(2,1)} %copy-done.7) | copy-start | bytes 245764
  107.6 3.7 %copy-start.36 = (bf16[10,1,256]{2,1,0:T(2,128)(2,1)S(1)}, bf16[10,1,256]{2,1,0:T(2,128)(2,1)}, u32[]{:S(2)}) copy-start(bf16[10,1,256]{2,1,0:T(2,128)(2,1)} %copy-done.35) | copy-start | bytes 15364
  107.6 4.6 %copy-start.33 = (bf16[10,1,256]{2,1,0:T(2,128)(2,1)S(1)}, bf16[10,1,256]{2,1,0:T(2,128)(2,1)}, u32[]{:S(2)}) copy-start(bf16[10,1,256]{2,1,0:T(2,128)(2,1)} %copy-done.32) | copy-start | bytes 15364
  109.5 3.7 %copy-start.25 = (bf16[8,16,256]{2,1,0:T(8,128)(2,1)S(1)}, bf16[8,16,256]{2,1,0:T(8,128)(2,1)}, u32[]{:S(2)}) copy-start(bf16[8,16,256]{2,1,0:T(8,128)(2,1)} %param.6) | copy-start | bytes 196612
  113.2 2.7 copy-start.27
  135.3 2.2 copy-start.2
  138.2 5.4 %collective-permute-start.10 = (bf16[10,1,256]{2,1,0:T(2,128)(2,1)S(1)}, bf16[10,1,256]{2,1,0:T(2,128)(2,1)S(1)}, u32[]{:S(2)}, u32[]{:S(2)}) collective-permute-start(bf16[10,1,256]{2,1,0:T(2,128)(2,1)S(1)} %get-tuple-element.28), channel_id=1, source_target_pairs={{1,0},{2,1},{3,2},{0,3},{5,4},{6,5},{7,6},{4,7},{9,8},{10,9},{11,1... | collective-permute-start | bytes 15368 | tf_op jit(solution)/shard_map/ppermute | solution.py:18
  138.3 5.4 %collective-permute-start.11 = (bf16[10,1,256]{2,1,0:T(2,128)(2,1)S(1)}, bf16[10,1,256]{2,1,0:T(2,128)(2,1)S(1)}, u32[]{:S(2)}, u32[]{:S(2)}) collective-permute-start(bf16[10,1,256]{2,1,0:T(2,128)(2,1)S(1)} %get-tuple-element.29), channel_id=1, source_target_pairs={{0,1},{1,2},{2,3},{3,0},{4,5},{5,6},{6,7},{7,4},{8,9},{9,10},{10,1... | collective-permute-start | bytes 15368 | tf_op jit(solution)/shard_map/ppermute | solution.py:16
  144.5 4.3 %copy-start.9 = (bf16[10,17,256]{2,1,0:T(8,128)(2,1)}, bf16[10,17,256]{2,1,0:T(8,128)(2,1)S(1)}, u32[]{:S(2)}) copy-start(bf16[10,17,256]{2,1,0:T(8,128)(2,1)S(1)} %get-tuple-element.26) | copy-start | bytes 261124
  144.5 4.5 %copy-start.11 = (bf16[10,17,256]{2,1,0:T(8,128)(2,1)}, bf16[10,17,256]{2,1,0:T(8,128)(2,1)S(1)}, u32[]{:S(2)}) copy-start(bf16[10,17,256]{2,1,0:T(8,128)(2,1)S(1)} %get-tuple-element.27) | copy-start | bytes 261124
  144.7 4.0 %copy-start.15 = (f32[8,16,256]{2,1,0:T(8,128)S(1)}, f32[8,16,256]{2,1,0:T(8,128)}, u32[]{:S(2)}) copy-start(f32[8,16,256]{2,1,0:T(8,128)} %fusion.104) | copy-start | bytes 393220
  145.1 3.9 %copy-start.28 = (f32[10,18,256]{2,1,0:T(8,128)S(1)}, f32[10,18,256]{2,1,0:T(8,128)}, u32[]{:S(2)}) copy-start(f32[10,18,256]{2,1,0:T(8,128)} %get-tuple-element.48) | copy-start | bytes 552964
  147.9 4.4 %copy-start.4 = (bf16[12,16,256]{2,1,0:T(8,128)(2,1)S(1)}, bf16[12,16,256]{2,1,0:T(8,128)(2,1)}, u32[]{:S(2)}) copy-start(bf16[12,16,256]{2,1,0:T(8,128)(2,1)} %copy-done.3) | copy-start | bytes 294916
  149.0 4.3 %copy-start.23 = (bf16[8,16,256]{2,1,0:T(8,128)(2,1)S(1)}, bf16[8,16,256]{2,1,0:T(8,128)(2,1)}, u32[]{:S(2)}) copy-start(bf16[8,16,256]{2,1,0:T(8,128)(2,1)} %param.5) | copy-start | bytes 196612
  149.0 5.9 %copy-start.30 = (bf16[12,2,256]{2,1,0:T(2,128)(2,1)S(1)}, bf16[12,2,256]{2,1,0:T(2,128)(2,1)}, u32[]{:S(2)}) copy-start(bf16[12,2,256]{2,1,0:T(2,128)(2,1)} %copy-done.29) | copy-start | bytes 36868
  149.2 11.2 %copy-start.5 = (bf16[8,16,256]{2,1,0:T(8,128)(2,1)}, bf16[8,16,256]{2,1,0:T(8,128)(2,1)S(1)}, u32[]{:S(2)}) copy-start(bf16[8,16,256]{2,1,0:T(8,128)(2,1)S(1)} %fusion.64) | copy-start | bytes 196612
  149.2 30.1 %collective-permute-start.13 = (bf16[1,16,256]{2,1,0:T(8,128)(2,1)S(1)}, bf16[1,16,256]{2,1,0:T(8,128)(2,1)S(1)}, u32[]{:S(2)}, u32[]{:S(2)}) collective-permute-start(bf16[1,16,256]{2,1,0:T(8,128)(2,1)S(1)} %get-tuple-element.33), channel_id=1, source_target_pairs={{4,0},{8,4},{12,8},{16,12},{20,16},{24,20},{28,24},{0,28},{5,1},{9... | collective-permute-start | bytes 24584 | tf_op jit(solution)/shard_map/ppermute | solution.py:18
  152.3 27.0 %collective-permute-start.12 = (bf16[1,16,256]{2,1,0:T(8,128)(2,1)S(1)}, bf16[1,16,256]{2,1,0:T(8,128)(2,1)S(1)}, u32[]{:S(2)}, u32[]{:S(2)}) collective-permute-start(bf16[1,16,256]{2,1,0:T(8,128)(2,1)S(1)} %get-tuple-element.32), channel_id=1, source_target_pairs={{0,4},{4,8},{8,12},{12,16},{16,20},{20,24},{24,28},{28,0},{1,5},{5... | collective-permute-start | bytes 24584 | tf_op jit(solution)/shard_map/ppermute | solution.py:16
  156.7 2.8 copy-start.38
  168.0 8.9 %copy-start.10 = (bf16[10,17,256]{2,1,0:T(8,128)(2,1)S(1)}, bf16[10,17,256]{2,1,0:T(8,128)(2,1)}, u32[]{:S(2)}) copy-start(bf16[10,17,256]{2,1,0:T(8,128)(2,1)} %copy-done.9) | copy-start | bytes 261124
  168.0 8.9 %copy-start.14 = (f32[8,16,256]{2,1,0:T(8,128)S(1)}, f32[8,16,256]{2,1,0:T(8,128)}, u32[]{:S(2)}) copy-start(f32[8,16,256]{2,1,0:T(8,128)} %fusion.81) | copy-start | bytes 393220
  168.0 8.9 %copy-start.18 = (f32[8,16,256]{2,1,0:T(8,128)S(1)}, f32[8,16,256]{2,1,0:T(8,128)}, u32[]{:S(2)}) copy-start(f32[8,16,256]{2,1,0:T(8,128)} %fusion.79) | copy-start | bytes 393220
  168.1 8.9 %copy-start.19 = (f32[8,16,256]{2,1,0:T(8,128)S(1)}, f32[8,16,256]{2,1,0:T(8,128)}, u32[]{:S(2)}) copy-start(f32[8,16,256]{2,1,0:T(8,128)} %fusion.77) | copy-start | bytes 393220
  176.9 1.3 copy-start.12
  176.9 1.3 copy-start.16
  176.9 1.3 copy-start.17
  176.9 1.3 copy-start.20
  176.9 2.2 copy-start.6
  179.3 2.7 collective-permute-start.14
  180.6 3.1 collective-permute-start.15
  308.3 1.9 copy-start.21
Sparse Core Ops, SparseCore 0:
  177.1 131.1 all-reduce.2
where the time goes:
time: 320 us; the launch traced here: 318 us
  waiting for transfers between devices  131 us (41%)
  matrix products  85.3 us (27%)
  local copies, waits for them, and re-layouts  64.6 us (20%)
  starting transfers between devices  18.4 us (6%)
  between operations  14.9 us (5%)
  other arithmetic  3.86 us (1%)
    psum x1, waiting for transfers between devices, body(): enc_total, dec_total = lax.psum((enc_terms, dec_terms), ('gx', 'gy'))  123 us
    convert_element_type x6, local copies, waits for them, and re-layouts, make_bands(): band.reshape(3, 3, planes * width_in, planes * width_out)  30.1 us
    dot_general x27, matrix products, tap_sums(): lax.dot_general(piece, flat_delta, (((0,), (0,)), ((), ())), preferred_el...  27.3 us
    dot_general x3, matrix products, tap_sums(): jnp.einsum('abpizo,cpz->abcio', stacked, shift_table(planes), precision=l...  26.4 us
    reshape x3, local copies, waits for them, and re-layouts, tap_sums(): jnp.stack(blocks).reshape(3, 3, planes, width_in, planes, width_out)  20.2 us
    dot_general x27, matrix products, band_conv_back(): jnp.dot(piece, band[shift_x, shift_y].T, preferred_element_type=jnp.float32)  15.6 us
    ppermute x8, starting transfers between devices, extended(): lax.ppermute(head, axis, [((i + 1) % count, i) for i in range(count)])  12.7 us
    dot_general x3, matrix products, make_bands(): jnp.einsum('cpz,abcio->abpizo', shift_table(planes), weight.astype(jnp.fl...  9.82 us
  transfers between devices with their start and end apart: 17, of which 6 were waited for; matrix products, arithmetic and copies ran while one was open for 43% of the time, Pallas kernels for 0%

commit v1 on v0

v1 whole, which is shorter than its diff:
```python
import functools
import math

import jax
import jax.numpy as jnp
from jax import lax
from jax.experimental import pallas as pl
from jax.experimental.pallas import tpu as pltpu
from jax.sharding import PartitionSpec as P

MESH = pl.DeviceIdType.MESH
F32 = jnp.float32
BF16 = jnp.bfloat16
BASE = 16
DIRECTIONS = [(dx, dy) for dx in (-1, 0, 1) for dy in (-1, 0, 1) if (dx, dy) != (0, 0)]


def sigmoid(value):
    return 1.0 / (1.0 + jnp.exp(-value))


def slope(value):
    sig = sigmoid(value)
    return sig * (1.0 + value * (1.0 - sig))


def kernel(
    nx, ny, scale,
    inputs, coarse, cotangent, enc_w, dec_w,
    inputs_grad, coarse_grad, enc_out, dec_out,
    enc_band, dec_band,
    mid_in, lo_in, hi_in, slo_in, shi_in,
    mid_co, lo_co, hi_co, slo_co, shi_co,
    mid_de, lo_de, hi_de, slo_de, shi_de,
    mid_en, lo_en, hi_en, slo_en, shi_en,
    wide, ext, near_in, near_co, near_sk, near_de, near_en,
    pre, acc_dec, acc_cat,
    g_dec, r1_dec, h_dec, r2_dec, f_dec,
    g_enc, r1_enc, h_enc, r2_enc, f_enc,
    halo_send, halo_recv, y_sems, x_sems,
):
    ix = lax.axis_index("gx")
    jy = lax.axis_index("gy")
    cx, cy, width = inputs.shape
    cells = cx * cy
    channels = enc_w.shape[2]
    planes = width // channels
    groups = 128 // channels

    def peer(dx, dy):
        return (lax.rem(ix + dx + nx, nx), lax.rem(jy + dy + ny, ny))

    partners = {(dx % nx, dy % ny) for dx, dy in DIRECTIONS}
    partners |= {(k, 0) for k in range(1, nx)} | {(0, k) for k in range(1, ny)}
    barrier = pltpu.get_barrier_semaphore()
    for dx, dy in sorted(partners):
        pl.semaphore_signal(barrier, inc=1, device_id=peer(dx, dy), device_id_type=MESH)

    def stage(value, w, slo, shi):
        slo[...] = value[:, 0:w].astype(F32)
        shi[...] = value[:, cy - w : cy].astype(F32)

    def halo(which, w, mid, lo, hi, slo, shi):
        src_x = {-1: (0, w), 0: (0, cx), 1: (cx - w, w)}
        dst_x = {-1: (cx + w, w), 0: (w, cx), 1: (0, w)}
        copies = []
        for d, (dx, dy) in enumerate(DIRECTIONS):
            start, size = src_x[dx]
            if dy == 0:
                source = mid.at[pl.ds(w + start, size)]
            else:
                source = (slo if dy < 0 else shi).at[pl.ds(start, size)]
            target = {0: mid, -1: hi, 1: lo}[dy].at[pl.ds(dst_x[dx][0], size)]
            copies.append(
                pltpu.make_async_remote_copy(
                    src_ref=source,
                    dst_ref=target,
                    send_sem=halo_send.at[which, d],
                    recv_sem=halo_recv.at[which, d],
                    device_id=peer(dx, dy),
                    device_id_type=MESH,
                )
            )
        return copies

    def start(copies):
        for copy in copies:
            copy.start()

    def arrive(copies):
        for copy in copies:
            copy.wait_recv()

    def fill(target, w, mid, lo, hi):
        target[:, BASE : BASE + cy] = mid[...].astype(F32)
        target[:, BASE - w : BASE] = lo[...]
        target[:, BASE + cy : BASE + cy + w] = hi[...]

    def spread(source, near):
        for b in range(3):
            near[b] = source[:, BASE - 1 + b : BASE - 1 + b + cy].astype(BF16)

    own_in = inputs[...]
    own_co = coarse[...]
    mid_in[2 : 2 + cx] = own_in
    mid_co[1 : 1 + cx] = own_co
    stage(own_in, 2, slo_in, shi_in)
    stage(own_co, 1, slo_co, shi_co)
    pl.semaphore_wait(barrier, len(partners))
    halo_in = halo(0, 2, mid_in, lo_in, hi_in, slo_in, shi_in)
    halo_co = halo(1, 1, mid_co, lo_co, hi_co, slo_co, shi_co)
    start(halo_in)
    start(halo_co)

    spread_mat = (
        lax.broadcasted_iota(jnp.int32, (channels, width), 1) % channels
        == lax.broadcasted_iota(jnp.int32, (channels, width), 0)
    ).astype(F32).astype(BF16)
    plane_of = lax.broadcasted_iota(jnp.int32, (channels, width), 1) // channels

    def band_block(taps, p):
        block = jnp.where(plane_of == p - 1, taps[2], 0.0)
        block = jnp.where(plane_of == p, taps[1], block)
        return jnp.where(plane_of == p + 1, taps[0], block).astype(BF16)

    def make_bands(t, carry):
        enc = jnp.dot(enc_w[t], spread_mat, preferred_element_type=F32)
        dec = jnp.dot(dec_w[t], spread_mat, preferred_element_type=F32)
        enc_taps = [enc[c * channels : (c + 1) * channels] for c in range(3)]
        dec_taps = [
            [dec[(2 * c + s) * channels : (2 * c + s + 1) * channels] for c in range(3)]
            for s in range(2)
        ]
        for p in range(planes):
            rows = slice(p * channels, (p + 1) * channels)
            enc_band[t, rows] = band_block(enc_taps, p)
            for s in range(2):
                dec_band[t, s * width + p * channels : s * width + (p + 1) * channels] = band_block(
                    dec_taps[s], p
                )
        return carry

    lax.fori_loop(0, 9, make_bands, 0)

    wide[...] = jnp.zeros_like(wide)
    pre[...] = jnp.zeros_like(pre)
    acc_dec[...] = jnp.zeros_like(acc_dec)
    acc_cat[...] = jnp.zeros_like(acc_cat)
    g_dec[...] = jnp.zeros_like(g_dec)
    g_enc[...] = jnp.zeros_like(g_enc)

    arrive(halo_in)
    fill(wide, 2, mid_in, lo_in, hi_in)
    for b in range(3):
        near_in[b, :, 0:cy] = wide[:, BASE - 1 + b : BASE - 1 + b + cy].astype(BF16)
        tail = jnp.concatenate(
            [
                wide[:, BASE + cy - 1 + b : BASE + cy + 7 + b],
                wide[:, BASE - 9 + b : BASE - 1 + b],
            ],
            axis=1,
        )
        near_in[b, :, cy : cy + 16] = tail.astype(BF16)

    def enc_step(t, carry):
        a, b = t // 3, t % 3
        piece = near_in[b, pl.ds(a, cx + 2)].reshape((cx + 2) * (cy + 16), width)
        pre[...] += jnp.dot(piece, enc_band[t], preferred_element_type=F32)
        return carry

    lax.fori_loop(0, 9, enc_step, 0)

    value = pre[...].reshape(cx + 2, cy + 16, width)
    skip = (value * sigmoid(value)).astype(BF16).astype(F32)
    ext[:, BASE : BASE + cy] = skip[:, 0:cy]
    ext[:, BASE + cy : BASE + cy + 8] = skip[:, cy : cy + 8]
    ext[:, BASE - 8 : BASE] = skip[:, cy + 8 : cy + 16]
    spread(ext, near_sk)

    arrive(halo_co)
    fill(ext, 1, mid_co, lo_co, hi_co)
    spread(ext, near_co)

    def tap(near, t):
        a, b = t // 3, t % 3
        return near[b, pl.ds(a, cx)].reshape(cells, width)

    def tap_back(near, t):
        a, b = t // 3, t % 3
        return near[2 - b, pl.ds(2 - a, cx)].reshape(cells, width)

    def dec_step(t, carry):
        acc_dec[...] += jnp.dot(
            tap(near_co, t), dec_band[t, 0:width], preferred_element_type=F32
        ) + jnp.dot(tap(near_sk, t), dec_band[t, width : 2 * width], preferred_element_type=F32)
        return carry

    lax.fori_loop(0, 9, dec_step, 0)

    dec_own = (cotangent[...].astype(F32).reshape(cells, width) * slope(acc_dec[...])).astype(BF16)
    dec_cells = dec_own.reshape(cx, cy, width)
    mid_de[1 : 1 + cx] = dec_cells
    stage(dec_cells, 1, slo_de, shi_de)
    halo_de = halo(2, 1, mid_de, lo_de, hi_de, slo_de, shi_de)
    start(halo_de)

    group_of = lax.broadcasted_iota(jnp.int32, (channels, 128), 1) // channels
    row_group = lax.broadcasted_iota(jnp.int32, (8, 128), 1) // channels

    def by_group(index, parts):
        out = parts[-1]
        for g in range(len(parts) - 2, -1, -1):
            out = jnp.where(index == g, parts[g], out)
        return out

    def fold(product, c):
        parts = []
        for g in range(groups):
            total = None
            for z in range(g, planes, groups):
                p = z + c - 1
                if 0 <= p < planes:
                    lane = (z // groups) * 128
                    term = product[p * channels : (p + 1) * channels, lane : lane + 128]
                    total = term if total is None else total + term
            parts.append(total)
        both = by_group(group_of, parts)
        step = 64
        while step >= channels:
            both = both + pltpu.roll(both, step, 1)
            step //= 2
        return by_group(row_group, [both[8 * g : 8 * g + 8] for g in range(groups)])

    def contract(piece, delta):
        return lax.dot_general(piece, delta, (((0,), (0,)), ((), ())), preferred_element_type=F32)

    def dec_taps_step(t, carry):
        delta = mid_de[1 : 1 + cx].reshape(cells, width)
        for s, near in enumerate((near_co, near_sk)):
            product = contract(tap(near, t), delta)
            for c in range(3):
                g_dec[(t * 3 + c) * 2 + s] = fold(product, c)
        return carry

    lax.fori_loop(0, 9, dec_taps_step, 0)

    class Reduce:
        def __init__(self, which, g, r1, h, r2, f):
            self.g, self.r1, self.h, self.r2, self.f = g, r1, h, r2, f
            self.p1 = h.shape[0]
            self.p2 = r2.shape[1]
            mine = jy * self.p1 + ix * self.p2
            self.mine = mine
            self.y_scatter = []
            self.y_gather = []
            for k in range(1, ny):
                there = lax.rem(jy + k, ny)
                for phase, src, dst in (
                    (0, g.at[pl.ds(there * self.p1, self.p1)], r1.at[k - 1]),
                    (1, f.at[pl.ds(jy * self.p1, self.p1)], f.at[pl.ds(jy * self.p1, self.p1)]),
                ):
                    (self.y_scatter, self.y_gather)[phase].append(
                        pltpu.make_async_remote_copy(
                            src_ref=src,
                            dst_ref=dst,
                            send_sem=y_sems.at[which, phase, 0, k - 1],
                            recv_sem=y_sems.at[which, phase, 1, k - 1],
                            device_id=(ix, there),
                            device_id_type=MESH,
                        )
                    )
            self.x_scatter = []
            self.x_gather = []
            for k in range(1, nx):
                there = lax.rem(ix + k, nx)
                for phase, src, dst in (
                    (0, h.at[pl.ds(there * self.p2, self.p2)], r2.at[k - 1]),
                    (1, f.at[pl.ds(mine, self.p2)], f.at[pl.ds(mine, self.p2)]),
                ):
                    (self.x_scatter, self.x_gather)[phase].append(
                        pltpu.make_async_remote_copy(
                            src_ref=src,
                            dst_ref=dst,
                            send_sem=x_sems.at[which, phase, 0, k - 1],
                            recv_sem=x_sems.at[which, phase, 1, k - 1],
                            device_id=(there, jy),
                            device_id_type=MESH,
                        )
                    )

        def step1(self):
            start(self.y_scatter)

        def step2(self):
            arrive(self.y_scatter)
            total = self.g[pl.ds(jy * self.p1, self.p1)]
            for k in range(ny - 1):
                total = total + self.r1[k]
            self.h[...] = total
            start(self.x_scatter)

        def step3(self):
            arrive(self.x_scatter)
            total = self.h[pl.ds(ix * self.p2, self.p2)]
            for k in range(nx - 1):
                total = total + self.r2[k]
            self.f[pl.ds(self.mine, self.p2)] = total * scale
            start(self.x_gather)

        def step4(self):
            arrive(self.x_gather)
            start(self.y_gather)

        def step5(self):
            arrive(self.y_gather)

        def drain(self):
            for copy in self.y_scatter + self.x_scatter + self.x_gather + self.y_gather:
                copy.wait_send()

    dec_sum = Reduce(0, g_dec, r1_dec, h_dec, r2_dec, f_dec)
    enc_sum = Reduce(1, g_enc, r1_enc, h_enc, r2_enc, f_enc)
    dec_sum.step1()

    arrive(halo_de)
    fill(ext, 1, mid_de, lo_de, hi_de)
    spread(ext, near_de)

    def cat_step(t, carry):
        acc_cat[...] += lax.dot_general(
            tap_back(near_de, t), dec_band[t], (((1,), (1,)), ((), ())), preferred_element_type=F32
        )
        return carry

    lax.fori_loop(0, 9, cat_step, 0)
    coarse_grad[...] = acc_cat[:, 0:width].astype(BF16).reshape(cx, cy, width)
    pre_own = pre[...].reshape(cx + 2, cy + 16, width)[1 : 1 + cx, 0:cy].reshape(cells, width)
    enc_own = (acc_cat[:, width : 2 * width] * slope(pre_own)).astype(BF16)
    enc_cells = enc_own.reshape(cx, cy, width)
    mid_en[1 : 1 + cx] = enc_cells
    stage(enc_cells, 1, slo_en, shi_en)
    halo_en = halo(3, 1, mid_en, lo_en, hi_en, slo_en, shi_en)
    start(halo_en)
    dec_sum.step2()

    def enc_taps_step(t, carry):
        a, b = t // 3, t % 3
        delta = mid_en[1 : 1 + cx].reshape(cells, width)
        piece = near_in[b, pl.ds(a + 1, cx), 0:cy].reshape(cells, width)
        product = contract(piece, delta)
        for c in range(3):
            g_enc[t * 3 + c] = fold(product, c)
        return carry

    lax.fori_loop(0, 9, enc_taps_step, 0)
    enc_sum.step1()
    dec_sum.step3()

    arrive(halo_en)
    fill(ext, 1, mid_en, lo_en, hi_en)
    spread(ext, near_en)
    enc_sum.step2()
    acc_dec[...] = jnp.zeros_like(acc_dec)

    def back_step(t, carry):
        acc_dec[...] += lax.dot_general(
            tap_back(near_en, t), enc_band[t], (((1,), (1,)), ((), ())), preferred_element_type=F32
        )
        return carry

    lax.fori_loop(0, 9, back_step, 0)
    inputs_grad[...] = acc_dec[...].astype(BF16).reshape(cx, cy, width)

    enc_sum.step3()
    dec_sum.step4()
    enc_sum.step4()
    dec_sum.step5()

    def unpack_dec(t, carry):
        tile = f_dec[t]
        for g in range(groups):
            dec_out[t, g] = tile[:, g * channels : (g + 1) * channels]
        return carry

    lax.fori_loop(0, dec_out.shape[0], unpack_dec, 0)
    enc_sum.step5()

    def unpack_enc(t, carry):
        tile = f_enc[t]
        for g in range(groups):
            enc_out[t, g] = tile[:, g * channels : (g + 1) * channels]
        return carry

    lax.fori_loop(0, enc_out.shape[0], unpack_enc, 0)

    for copies in (halo_in, halo_co, halo_de, halo_en):
        for copy in copies:
            copy.wait_send()
    dec_sum.drain()
    enc_sum.drain()


def body(nx, ny, inputs, coarse, cotangent, enc_weight, dec_weight):
    cx, cy, width = inputs.shape
    channels = enc_weight.shape[3]
    planes = width // channels
    groups = 128 // channels
    rows = channels // groups
    cells = cx * cy
    scale = 1.0 / math.sqrt(cx * nx * cy * ny * planes)

    def halo_buffers(w):
        return [
            pltpu.VMEM((cx + 2 * w, cy, width), BF16),
            pltpu.VMEM((cx + 2 * w, w, width), F32),
            pltpu.VMEM((cx + 2 * w, w, width), F32),
            pltpu.VMEM((cx, w, width), F32),
            pltpu.VMEM((cx, w, width), F32),
        ]

    def sum_buffers(tiles):
        p2 = -(-tiles // (nx * ny))
        p1 = p2 * nx
        return [
            pltpu.VMEM((p1 * ny, 8, 128), F32),
            pltpu.VMEM((ny - 1, p1, 8, 128), F32),
            pltpu.VMEM((p1, 8, 128), F32),
            pltpu.VMEM((nx - 1, p2, 8, 128), F32),
            pltpu.VMEM((p1 * ny, 8, 128), F32),
        ]

    near = pltpu.VMEM((3, cx + 2, cy, width), BF16)
    vmem = pl.BlockSpec(memory_space=pltpu.VMEM)
    inputs_grad, coarse_grad, enc_total, dec_total = pl.pallas_call(
        functools.partial(kernel, nx, ny, scale),
        out_shape=(
            jax.ShapeDtypeStruct((cx, cy, width), BF16),
            jax.ShapeDtypeStruct((cx, cy, width), BF16),
            jax.ShapeDtypeStruct((27, groups, rows, channels), F32),
            jax.ShapeDtypeStruct((54, groups, rows, channels), F32),
        ),
        in_specs=[vmem] * 5,
        out_specs=(vmem,) * 4,
        scratch_shapes=[
            pltpu.VMEM((9, width, width), BF16),
            pltpu.VMEM((9, 2 * width, width), BF16),
            *halo_buffers(2),
            *halo_buffers(1),
            *halo_buffers(1),
            *halo_buffers(1),
            pltpu.VMEM((cx + 4, cy + 32, width), F32),
            pltpu.VMEM((cx + 2, cy + 32, width), F32),
            pltpu.VMEM((3, cx + 4, cy + 16, width), BF16),
            near,
            near,
            near,
            near,
            pltpu.VMEM(((cx + 2) * (cy + 16), width), F32),
            pltpu.VMEM((cells, width), F32),
            pltpu.VMEM((cells, 2 * width), F32),
            *sum_buffers(54),
            *sum_buffers(27),
            pltpu.SemaphoreType.DMA((4, 8)),
            pltpu.SemaphoreType.DMA((4, 8)),
            pltpu.SemaphoreType.DMA((2, 2, 2, ny - 1)),
            pltpu.SemaphoreType.DMA((2, 2, 2, nx - 1)),
        ],
        compiler_params=pltpu.CompilerParams(
            collective_id=0, has_side_effects=True, vmem_limit_bytes=48 << 20
        ),
    )(
        inputs,
        coarse,
        cotangent,
        enc_weight.reshape(9, 3 * channels, channels),
        dec_weight.reshape(9, 6 * channels, channels),
    )
    return (
        inputs_grad,
        coarse_grad,
        enc_total.reshape(3, 3, 3, channels, channels),
        dec_total.reshape(3, 3, 3, 2 * channels, channels),
    )


def solution(mesh):
    in_specs = (P("gx", "gy", None), P("gx", "gy", None), P("gx", "gy", None), P(), P())
    out_specs = (P("gx", "gy", None), P("gx", "gy", None), P(), P())
    return jax.shard_map(
        functools.partial(body, mesh.shape["gx"], mesh.shape["gy"]),
        mesh=mesh,
        in_specs=in_specs,
        out_specs=out_specs,
        check_vma=False,
    )
```

time: 320 us -> 50.5 us (0.16)
  waiting for transfers between devices: 131 us -> 0 us
  matrix products: 85.3 us -> 0 us
  local copies, waits for them, and re-layouts: 64.6 us -> 4.32 us
  Pallas kernels: 0 us -> 44.5 us
  starting transfers between devices: 18.4 us -> 0 us
  between operations: 14.9 us -> 0.71 us
  other arithmetic: 3.86 us -> 0 us
    psum x1 -> x0, waiting for transfers between devices: 123 us -> none  [body(): enc_total, dec_total = lax.psum((enc_terms, dec_terms), ('gx', 'gy'))]
    dot_general x87 -> x0, matrix products: 85.3 us -> none  [the longest x27 27.3 us: tap_sums(): lax.dot_general(piece, flat_delta, (((0,), (0,)), ((), ())), preferred_el...]
    pallas_call x0 -> x1, Pallas kernels: none -> 44.5 us  [body(): pl.pallas_call(functools.partial(kernel, nx, ny, scale), out_shape=(jax.S...]
    convert_element_type x6 -> x0, local copies, waits for them, and re-layouts: 30.1 us -> none  [make_bands(): band.reshape(3, 3, planes * width_in, planes * width_out)]
    reshape x3 -> x0, local copies, waits for them, and re-layouts: 20.2 us -> none  [tap_sums(): jnp.stack(blocks).reshape(3, 3, planes, width_in, planes, width_out)]
    ppermute x16 -> x0, starting transfers between devices: 18.3 us -> none  [the longest x8 12.7 us: extended(): lax.ppermute(head, axis, [((i + 1) % count, i) for i in range(count)])]
    ppermute x16 -> x0, waiting for transfers between devices: 8.21 us -> none  [the longest x8 6.48 us: extended(): lax.ppermute(tail, axis, [(i, (i + 1) % count) for i in range(count)])]
    transpose x2 -> x0, local copies, waits for them, and re-layouts: 4.02 us -> none  [tap_sums(): jnp.einsum('abpizo,cpz->abcio', stacked, shift_table(planes), precision=l...]
  transfers between devices with their start and end apart: 17 -> 0, of which waited for: 6 -> 0; matrix products, arithmetic and copies ran while one was open for 43% -> 0% of each run, Pallas kernels for 0% -> 0%
where the time goes in v1:
time: 50.5 us; the launch traced here: 49.5 us
  Pallas kernels  44.5 us (88%)
  local copies, waits for them, and re-layouts  4.32 us (9%)
  between operations  0.71 us (1%)
    pallas_call x1, Pallas kernels, body(): pl.pallas_call(functools.partial(kernel, nx, ny, scale), out_shape=(jax.S...  44.5 us
    unnamed x13, local copies, waits for them, and re-layouts  4.32 us

profile of v1, /device:TPU:0, one launch (start us, length us, event | category | flops | bytes accessed | tf_op | source)
XLA Modules:
  0.0 49.5 jit_solution(2806895847347008284)
XLA Ops:
  0.6 0.0 copy-start
  0.6 0.0 copy-start.1
  0.7 0.0 copy-start.2
  0.7 0.0 copy-start.3
  0.7 1.2 %copy.9 = bf16[3,3,3,64,32]{4,3,2,1,0:T(8,128)(2,1)S(1)} copy(bf16[3,3,3,64,32]{3,4,2,1,0:T(8,128)(2,1)} %param.9) | data formatting | bytes 221184 | tf_op args[4]
  1.9 0.0 copy-done
  1.9 0.0 copy-done.1
  1.9 0.0 copy-done.2
  1.9 0.0 copy-done.3
  1.9 44.5 %shard_map.84 = (bf16[8,16,256]{2,1,0:T(8,128)(2,1)S(1)}, bf16[8,16,256]{2,1,0:T(8,128)(2,1)S(1)}, f32[27,4,8,32]{3,2,1,0:T(8,128)S(1)}, f32[54,4,8,32]{3,2,1,0:T(8,128)S(1)}) custom-call(bf16[8,16,256]{2,1,0:T(8,128)(2,1)S(1)} %copy-done.1, bf16[8,16,256]{2,1,0:T(8,128)(2,1)S(1)} %copy-done.2, bf16[8,16,256]{2,1,0:T(8,128)(2,1)S(1)} %copy-done.3, ...), custom_call_target="tpu_custom_call" | custom-call | tf_op jit(solution)/shard_map/pallas_call | solution.py:434
  46.4 1.1 %copy.10 = f32[3,3,3,64,32]{3,4,2,1,0:T(8,128)} copy(f32[3,3,3,64,32]{4,3,2,1,0:T(8,128)S(1)} %bitcast.5) | data formatting | bytes 442368
  47.5 0.6 %copy.14 = bf16[8,16,256]{2,1,0:T(8,128)(2,1)} copy(bf16[8,16,256]{2,1,0:T(8,128)(2,1)S(1)} %get-tuple-element.20) | data formatting | bytes 131072
  48.1 0.6 %copy.15 = bf16[8,16,256]{2,1,0:T(8,128)(2,1)} copy(bf16[8,16,256]{2,1,0:T(8,128)(2,1)S(1)} %get-tuple-element.21) | data formatting | bytes 131072
  48.7 0.8 %copy.16 = f32[3,3,3,32,32]{4,3,2,1,0:T(8,128)} copy(f32[3,3,3,32,32]{4,3,2,1,0:T(8,128)S(1)} %bitcast.6) | data formatting | bytes 221184
Async XLA Ops:
  0.6 1.3 %copy-start = (bf16[3,3,3,32,32]{4,3,2,1,0:T(8,128)(2,1)S(1)}, bf16[3,3,3,32,32]{4,3,2,1,0:T(8,128)(2,1)}, u32[]{:S(2)}) copy-start(bf16[3,3,3,32,32]{4,3,2,1,0:T(8,128)(2,1)} %param.8) | copy-start | bytes 165892
  0.6 1.3 %copy-start.1 = (bf16[8,16,256]{2,1,0:T(8,128)(2,1)S(1)}, bf16[8,16,256]{2,1,0:T(8,128)(2,1)}, u32[]{:S(2)}) copy-start(bf16[8,16,256]{2,1,0:T(8,128)(2,1)} %inputs.1) | copy-start | bytes 196612
  0.7 1.3 %copy-start.2 = (bf16[8,16,256]{2,1,0:T(8,128)(2,1)S(1)}, bf16[8,16,256]{2,1,0:T(8,128)(2,1)}, u32[]{:S(2)}) copy-start(bf16[8,16,256]{2,1,0:T(8,128)(2,1)} %coarse.1) | copy-start | bytes 196612
  0.7 1.3 %copy-start.3 = (bf16[8,16,256]{2,1,0:T(8,128)(2,1)S(1)}, bf16[8,16,256]{2,1,0:T(8,128)(2,1)}, u32[]{:S(2)}) copy-start(bf16[8,16,256]{2,1,0:T(8,128)(2,1)} %cotangent.1) | copy-start | bytes 196612

commit v2 on v1

--- a/solution.py
+++ b/solution.py
@@ -140,7 +140,7 @@
                 )
         return carry
 
-    lax.fori_loop(0, 9, make_bands, 0)
+    lax.fori_loop(0, 9, make_bands, 0, unroll=9)
 
     wide[...] = jnp.zeros_like(wide)
     pre[...] = jnp.zeros_like(pre)
@@ -168,7 +168,7 @@
         pre[...] += jnp.dot(piece, enc_band[t], preferred_element_type=F32)
         return carry
 
-    lax.fori_loop(0, 9, enc_step, 0)
+    lax.fori_loop(0, 9, enc_step, 0, unroll=9)
 
     value = pre[...].reshape(cx + 2, cy + 16, width)
     skip = (value * sigmoid(value)).astype(BF16).astype(F32)
@@ -195,7 +195,7 @@
         ) + jnp.dot(tap(near_sk, t), dec_band[t, width : 2 * width], preferred_element_type=F32)
         return carry
 
-    lax.fori_loop(0, 9, dec_step, 0)
+    lax.fori_loop(0, 9, dec_step, 0, unroll=9)
 
     dec_own = (cotangent[...].astype(F32).reshape(cells, width) * slope(acc_dec[...])).astype(BF16)
     dec_cells = dec_own.reshape(cx, cy, width)
@@ -242,7 +242,7 @@
                 g_dec[(t * 3 + c) * 2 + s] = fold(product, c)
         return carry
 
-    lax.fori_loop(0, 9, dec_taps_step, 0)
+    lax.fori_loop(0, 9, dec_taps_step, 0, unroll=9)
 
     class Reduce:
         def __init__(self, which, g, r1, h, r2, f):
@@ -332,7 +332,7 @@
         )
         return carry
 
-    lax.fori_loop(0, 9, cat_step, 0)
+    lax.fori_loop(0, 9, cat_step, 0, unroll=9)
     coarse_grad[...] = acc_cat[:, 0:width].astype(BF16).reshape(cx, cy, width)
     pre_own = pre[...].reshape(cx + 2, cy + 16, width)[1 : 1 + cx, 0:cy].reshape(cells, width)
     enc_own = (acc_cat[:, width : 2 * width] * slope(pre_own)).astype(BF16)
@@ -352,7 +352,7 @@
             g_enc[t * 3 + c] = fold(product, c)
         return carry
 
-    lax.fori_loop(0, 9, enc_taps_step, 0)
+    lax.fori_loop(0, 9, enc_taps_step, 0, unroll=9)
     enc_sum.step1()
     dec_sum.step3()
 
@@ -368,7 +368,7 @@
         )
         return carry
 
-    lax.fori_loop(0, 9, back_step, 0)
+    lax.fori_loop(0, 9, back_step, 0, unroll=9)
     inputs_grad[...] = acc_dec[...].astype(BF16).reshape(cx, cy, width)
 
     enc_sum.step3()
@@ -382,7 +382,7 @@
             dec_out[t, g] = tile[:, g * channels : (g + 1) * channels]
         return carry
 
-    lax.fori_loop(0, dec_out.shape[0], unpack_dec, 0)
+    lax.fori_loop(0, dec_out.shape[0], unpack_dec, 0, unroll=True)
     enc_sum.step5()
 
     def unpack_enc(t, carry):
@@ -391,7 +391,7 @@
             enc_out[t, g] = tile[:, g * channels : (g + 1) * channels]
         return carry
 
-    lax.fori_loop(0, enc_out.shape[0], unpack_enc, 0)
+    lax.fori_loop(0, enc_out.shape[0], unpack_enc, 0, unroll=True)
 
     for copies in (halo_in, halo_co, halo_de, halo_en):
         for copy in copies:

time: 50.5 us -> 40.3 us (0.80); the launches traced: 49.5 us -> 40.2 us
  Pallas kernels: 44.5 us -> 35.2 us
    pallas_call x1, Pallas kernels: 44.5 us -> 35.2 us  [body(): pl.pallas_call(functools.partial(kernel, nx, ny, scale), out_shape=(jax.S...]
where the time goes in v2:
time: 40.3 us; the launch traced here: 40.2 us
  Pallas kernels  35.2 us (87%)
  local copies, waits for them, and re-layouts  4.32 us (11%)
  between operations  0.71 us (2%)
    pallas_call x1, Pallas kernels, body(): pl.pallas_call(functools.partial(kernel, nx, ny, scale), out_shape=(jax.S...  35.2 us
    unnamed x13, local copies, waits for them, and re-layouts  4.32 us

profile of v2, /device:TPU:0, one launch (start us, length us, event | category | flops | bytes accessed | tf_op | source)
XLA Modules:
  0.0 40.2 jit_solution(3062708013326800924)
XLA Ops:
  0.6 0.0 copy-start
  0.6 0.0 copy-start.1
  0.7 0.0 copy-start.2
  0.7 0.0 copy-start.3
  0.7 1.2 %copy.9 = bf16[3,3,3,64,32]{4,3,2,1,0:T(8,128)(2,1)S(1)} copy(bf16[3,3,3,64,32]{3,4,2,1,0:T(8,128)(2,1)} %param.9) | data formatting | bytes 221184 | tf_op args[4]
  1.9 0.0 copy-done
  1.9 0.0 copy-done.1
  1.9 0.0 copy-done.2
  1.9 0.0 copy-done.3
  1.9 35.2 %shard_map.84 = (bf16[8,16,256]{2,1,0:T(8,128)(2,1)S(1)}, bf16[8,16,256]{2,1,0:T(8,128)(2,1)S(1)}, f32[27,4,8,32]{3,2,1,0:T(8,128)S(1)}, f32[54,4,8,32]{3,2,1,0:T(8,128)S(1)}) custom-call(bf16[8,16,256]{2,1,0:T(8,128)(2,1)S(1)} %copy-done.1, bf16[8,16,256]{2,1,0:T(8,128)(2,1)S(1)} %copy-done.2, bf16[8,16,256]{2,1,0:T(8,128)(2,1)S(1)} %copy-done.3, ...), custom_call_target="tpu_custom_call" | custom-call | tf_op jit(solution)/shard_map/pallas_call | solution.py:434
  37.1 1.1 %copy.10 = f32[3,3,3,64,32]{3,4,2,1,0:T(8,128)} copy(f32[3,3,3,64,32]{4,3,2,1,0:T(8,128)S(1)} %bitcast.5) | data formatting | bytes 442368
  38.2 0.6 %copy.14 = bf16[8,16,256]{2,1,0:T(8,128)(2,1)} copy(bf16[8,16,256]{2,1,0:T(8,128)(2,1)S(1)} %get-tuple-element.20) | data formatting | bytes 131072
  38.8 0.6 %copy.15 = bf16[8,16,256]{2,1,0:T(8,128)(2,1)} copy(bf16[8,16,256]{2,1,0:T(8,128)(2,1)S(1)} %get-tuple-element.21) | data formatting | bytes 131072
  39.4 0.8 %copy.16 = f32[3,3,3,32,32]{4,3,2,1,0:T(8,128)} copy(f32[3,3,3,32,32]{4,3,2,1,0:T(8,128)S(1)} %bitcast.6) | data formatting | bytes 221184
Async XLA Ops:
  0.6 1.3 %copy-start = (bf16[3,3,3,32,32]{4,3,2,1,0:T(8,128)(2,1)S(1)}, bf16[3,3,3,32,32]{4,3,2,1,0:T(8,128)(2,1)}, u32[]{:S(2)}) copy-start(bf16[3,3,3,32,32]{4,3,2,1,0:T(8,128)(2,1)} %param.8) | copy-start | bytes 165892
  0.6 1.3 %copy-start.1 = (bf16[8,16,256]{2,1,0:T(8,128)(2,1)S(1)}, bf16[8,16,256]{2,1,0:T(8,128)(2,1)}, u32[]{:S(2)}) copy-start(bf16[8,16,256]{2,1,0:T(8,128)(2,1)} %inputs.1) | copy-start | bytes 196612
  0.7 1.3 %copy-start.2 = (bf16[8,16,256]{2,1,0:T(8,128)(2,1)S(1)}, bf16[8,16,256]{2,1,0:T(8,128)(2,1)}, u32[]{:S(2)}) copy-start(bf16[8,16,256]{2,1,0:T(8,128)(2,1)} %coarse.1) | copy-start | bytes 196612
  0.7 1.3 %copy-start.3 = (bf16[8,16,256]{2,1,0:T(8,128)(2,1)S(1)}, bf16[8,16,256]{2,1,0:T(8,128)(2,1)}, u32[]{:S(2)}) copy-start(bf16[8,16,256]{2,1,0:T(8,128)(2,1)} %cotangent.1) | copy-start | bytes 196612

commit v3 on v2

--- a/solution.py
+++ b/solution.py
@@ -371,9 +371,8 @@
     lax.fori_loop(0, 9, back_step, 0, unroll=9)
     inputs_grad[...] = acc_dec[...].astype(BF16).reshape(cx, cy, width)
 
+    dec_sum.step4()
     enc_sum.step3()
-    dec_sum.step4()
-    enc_sum.step4()
     dec_sum.step5()
 
     def unpack_dec(t, carry):
@@ -383,6 +382,7 @@
         return carry
 
     lax.fori_loop(0, dec_out.shape[0], unpack_dec, 0, unroll=True)
+    enc_sum.step4()
     enc_sum.step5()
 
     def unpack_enc(t, carry):

time: 40.3 us -> 40.7 us (level)
  no operation moved by 1% of the time
where the time goes in v3:
time: 40.7 us; the launch traced here: 40.5 us
  Pallas kernels  35.5 us (87%)
  local copies, waits for them, and re-layouts  4.32 us (11%)
  between operations  0.71 us (2%)
    pallas_call x1, Pallas kernels, body(): pl.pallas_call(functools.partial(kernel, nx, ny, scale), out_shape=(jax.S...  35.5 us
    unnamed x13, local copies, waits for them, and re-layouts  4.32 us

profile of v3, /device:TPU:0, one launch (start us, length us, event | category | flops | bytes accessed | tf_op | source)
XLA Modules:
  0.0 40.5 jit_solution(9510589237671058452)
XLA Ops:
  0.6 0.0 copy-start
  0.6 0.0 copy-start.1
  0.7 0.0 copy-start.2
  0.7 0.0 copy-start.3
  0.7 1.2 %copy.9 = bf16[3,3,3,64,32]{4,3,2,1,0:T(8,128)(2,1)S(1)} copy(bf16[3,3,3,64,32]{3,4,2,1,0:T(8,128)(2,1)} %param.9) | data formatting | bytes 221184 | tf_op args[4]
  1.9 0.0 copy-done
  1.9 0.0 copy-done.1
  1.9 0.0 copy-done.2
  1.9 0.0 copy-done.3
  1.9 35.5 %shard_map.84 = (bf16[8,16,256]{2,1,0:T(8,128)(2,1)S(1)}, bf16[8,16,256]{2,1,0:T(8,128)(2,1)S(1)}, f32[27,4,8,32]{3,2,1,0:T(8,128)S(1)}, f32[54,4,8,32]{3,2,1,0:T(8,128)S(1)}) custom-call(bf16[8,16,256]{2,1,0:T(8,128)(2,1)S(1)} %copy-done.1, bf16[8,16,256]{2,1,0:T(8,128)(2,1)S(1)} %copy-done.2, bf16[8,16,256]{2,1,0:T(8,128)(2,1)S(1)} %copy-done.3, ...), custom_call_target="tpu_custom_call" | custom-call | tf_op jit(solution)/shard_map/pallas_call | solution.py:434
  37.5 1.1 %copy.10 = f32[3,3,3,64,32]{3,4,2,1,0:T(8,128)} copy(f32[3,3,3,64,32]{4,3,2,1,0:T(8,128)S(1)} %bitcast.5) | data formatting | bytes 442368
  38.5 0.6 %copy.14 = bf16[8,16,256]{2,1,0:T(8,128)(2,1)} copy(bf16[8,16,256]{2,1,0:T(8,128)(2,1)S(1)} %get-tuple-element.20) | data formatting | bytes 131072
  39.1 0.6 %copy.15 = bf16[8,16,256]{2,1,0:T(8,128)(2,1)} copy(bf16[8,16,256]{2,1,0:T(8,128)(2,1)S(1)} %get-tuple-element.21) | data formatting | bytes 131072
  39.8 0.8 %copy.16 = f32[3,3,3,32,32]{4,3,2,1,0:T(8,128)} copy(f32[3,3,3,32,32]{4,3,2,1,0:T(8,128)S(1)} %bitcast.6) | data formatting | bytes 221184
Async XLA Ops:
  0.6 1.3 %copy-start = (bf16[3,3,3,32,32]{4,3,2,1,0:T(8,128)(2,1)S(1)}, bf16[3,3,3,32,32]{4,3,2,1,0:T(8,128)(2,1)}, u32[]{:S(2)}) copy-start(bf16[3,3,3,32,32]{4,3,2,1,0:T(8,128)(2,1)} %param.8) | copy-start | bytes 165892
  0.6 1.3 %copy-start.1 = (bf16[8,16,256]{2,1,0:T(8,128)(2,1)S(1)}, bf16[8,16,256]{2,1,0:T(8,128)(2,1)}, u32[]{:S(2)}) copy-start(bf16[8,16,256]{2,1,0:T(8,128)(2,1)} %inputs.1) | copy-start | bytes 196612
  0.7 1.3 %copy-start.2 = (bf16[8,16,256]{2,1,0:T(8,128)(2,1)S(1)}, bf16[8,16,256]{2,1,0:T(8,128)(2,1)}, u32[]{:S(2)}) copy-start(bf16[8,16,256]{2,1,0:T(8,128)(2,1)} %coarse.1) | copy-start | bytes 196612
  0.7 1.3 %copy-start.3 = (bf16[8,16,256]{2,1,0:T(8,128)(2,1)S(1)}, bf16[8,16,256]{2,1,0:T(8,128)(2,1)}, u32[]{:S(2)}) copy-start(bf16[8,16,256]{2,1,0:T(8,128)(2,1)} %cotangent.1) | copy-start | bytes 196612
